TPU v7x, 32 devices: a whole 2x2x4 slice. The times are simulated.
32 devices in a mesh: dp: 4 (over z), fsdp: 8 (over y, x, core).
Axes of the slice: x: 2, y: 2, z: 4, core: 2. Of those that a mesh axis runs over, the one named last changes fastest.
Arguments:
- frames: bfloat16 [256, 256, 512], P(('dp', 'fsdp')), may hold values from -6 to 6
- group: int32 [256], P(('dp', 'fsdp')), may hold values from 0 to 1
- lengths: int32 [256], P(('dp', 'fsdp')), may hold values from 128 to 256, as said below
- conv_weight: bfloat16 [2, 7, 512], P(None, None, ('dp', 'fsdp')), may hold values from -2 to 2
- conv_bias: bfloat16 [2, 512], P(None, ('dp', 'fsdp')), may hold values from -3 to 3
- ada_scale: bfloat16 [2, 2, 512], P(None, None, ('dp', 'fsdp')), may hold values from 0.5 to 1.5
- ada_shift: bfloat16 [2, 2, 512], P(None, None, ('dp', 'fsdp')), may hold values from -3 to 3
- up_weight: bfloat16 [2, 512, 1536], P(None, ('dp', 'fsdp')), may hold values from -0.25 to 0.25
- up_bias: bfloat16 [2, 1536], P(None, ('dp', 'fsdp')), may hold values from -3 to 3
- down_weight: bfloat16 [2, 1536, 512], P(None, ('dp', 'fsdp')), may hold values from -0.15625 to 0.15625
- down_bias: bfloat16 [2, 512], P(None, ('dp', 'fsdp')), may hold values from -3 to 3
- layer_scale: bfloat16 [2, 512], P(None, ('dp', 'fsdp')), may hold values from 0.5 to 1.5
- out_grad: bfloat16 [256, 256, 512], P(('dp', 'fsdp')), may hold values from -6 to 6
Outputs:
- output: bfloat16 [256, 256, 512], P(('dp', 'fsdp'))
- input_grad: float32 [256, 256, 512], P(('dp', 'fsdp'))
- conv_weight_grad: float32 [2, 7, 512], P(None, None, ('dp', 'fsdp'))
- conv_bias_grad: float32 [2, 512], P(None, ('dp', 'fsdp'))
- ada_scale_grad: float32 [2, 2, 512], P(None, None, ('dp', 'fsdp'))
- ada_shift_grad: float32 [2, 2, 512], P(None, None, ('dp', 'fsdp'))
- up_weight_grad: float32 [2, 512, 1536], P(None, ('dp', 'fsdp'))
- up_bias_grad: float32 [2, 1536], P(None, ('dp', 'fsdp'))
- down_weight_grad: float32 [2, 1536, 512], P(None, ('dp', 'fsdp'))
- down_bias_grad: float32 [2, 512], P(None, ('dp', 'fsdp'))
- layer_scale_grad: float32 [2, 512], P(None, ('dp', 'fsdp'))
Inputs may be any that keep to these rules, and one draw needn't show every extreme that they name: `lengths`: A clip of group 0 has at most 256 valid frames, one of group 1 at most 236; clip 0 has 256 and clip 1 has 236.
All inputs are finite; a program needn't handle non-finite values.
Results may differ from a plain program's by a relative error of at most 0.0066.
Values may be sent and summed in bfloat16 or wider, within the bound.
A program may use at most 192 MiB of HBM per device.

v0:
```python
from functools import partial
import jax
import jax.numpy as jnp
from jax import lax
from jax.sharding import PartitionSpec as P

EPSILON = 1e-06


def forward_block(fetched, stream, valid_rows, select):
    kernel_taps = fetched[0].astype(jnp.float32)
    conv_shift = fetched[1].astype(jnp.float32)
    scale_table = fetched[2].astype(jnp.float32)
    shift_table = fetched[3].astype(jnp.float32)
    up_matrix = fetched[4]
    up_offset = fetched[5].astype(jnp.float32)
    down_matrix = fetched[6]
    down_offset = fetched[7].astype(jnp.float32)
    layer_gain = fetched[8].astype(jnp.float32)
    clip_count, frame_count, model_width = stream.shape
    half_kernel = kernel_taps.shape[0] // 2
    masked = stream * valid_rows
    padded = jnp.pad(masked, ((0, 0), (half_kernel, half_kernel), (0, 0)))
    mixed = conv_shift
    for offset in range(kernel_taps.shape[0]):
        mixed = mixed + kernel_taps[offset] * padded[:, offset : offset + frame_count, :]
    center = mixed - jnp.mean(mixed, axis=-1, keepdims=True)
    spread = jnp.mean(center * center, axis=-1, keepdims=True)
    inv_std = lax.rsqrt(spread + EPSILON)
    normed = center * inv_std
    gain_rows = jnp.einsum("cg,gd->cd", select, scale_table, precision=lax.Precision.HIGHEST)
    shift_rows = jnp.einsum("cg,gd->cd", select, shift_table, precision=lax.Precision.HIGHEST)
    shaped = normed * gain_rows[:, None, :] + shift_rows[:, None, :]
    shaped_low = shaped.astype(jnp.bfloat16).reshape(clip_count * frame_count, model_width)
    before = jnp.dot(shaped_low, up_matrix, preferred_element_type=jnp.float32) + up_offset
    activated_low = jax.nn.gelu(before, approximate=False).astype(jnp.bfloat16)
    branch = jnp.dot(activated_low, down_matrix, preferred_element_type=jnp.float32) + down_offset
    branch = branch.reshape(clip_count, frame_count, model_width)
    output = stream + valid_rows * layer_gain * branch
    return (output, (padded, normed, inv_std, gain_rows, shaped_low, before, activated_low, branch))


def backward_block(fetched, saved_state, grad_stream, valid_rows, select):
    kernel_taps = fetched[0].astype(jnp.float32)
    up_matrix = fetched[4]
    down_matrix = fetched[6]
    layer_gain = fetched[8].astype(jnp.float32)
    padded, normed, inv_std, gain_rows, shaped_low, before, activated_low, branch = saved_state
    clip_count, frame_count, model_width = grad_stream.shape
    kernel_len = kernel_taps.shape[0]
    half_kernel = kernel_len // 2
    gain_term = jnp.sum(valid_rows * branch * grad_stream, axis=(0, 1))
    grad_branch = (valid_rows * layer_gain * grad_stream).astype(jnp.bfloat16)
    down_offset_term = jnp.sum(grad_branch.astype(jnp.float32), axis=(0, 1))
    branch_rows = grad_branch.reshape(clip_count * frame_count, model_width)
    down_term = jnp.einsum(
        "rh,rd->hd", activated_low, branch_rows, preferred_element_type=jnp.float32
    )
    grad_activated = jnp.einsum(
        "rd,hd->rh", branch_rows, down_matrix, preferred_element_type=jnp.float32
    )
    unused_value, gelu_pull = jax.vjp(partial(jax.nn.gelu, approximate=False), before)
    grad_before = gelu_pull(grad_activated)[0].astype(jnp.bfloat16)
    up_offset_term = jnp.sum(grad_before.astype(jnp.float32), axis=0)
    up_term = jnp.einsum("rd,rh->dh", shaped_low, grad_before, preferred_element_type=jnp.float32)
    grad_shaped = jnp.einsum(
        "rh,dh->rd", grad_before, up_matrix, preferred_element_type=jnp.float32
    )
    grad_shaped = grad_shaped.reshape(clip_count, frame_count, model_width)
    clip_scale = jnp.sum(grad_shaped * normed, axis=1)
    clip_shift = jnp.sum(grad_shaped, axis=1)
    scale_term = jnp.einsum("cg,cd->gd", select, clip_scale, precision=lax.Precision.HIGHEST)
    shift_term = jnp.einsum("cg,cd->gd", select, clip_shift, precision=lax.Precision.HIGHEST)
    grad_normed = grad_shaped * gain_rows[:, None, :]
    grad_mixed = inv_std * (
        grad_normed
        - jnp.mean(grad_normed, axis=-1, keepdims=True)
        - normed * jnp.mean(grad_normed * normed, axis=-1, keepdims=True)
    )
    conv_shift_term = jnp.sum(grad_mixed, axis=(0, 1))
    kernel_term = jnp.stack(
        [
            jnp.sum(grad_mixed * padded[:, offset : offset + frame_count, :], axis=(0, 1))
            for offset in range(kernel_len)
        ]
    )
    grad_padded = jnp.pad(grad_mixed, ((0, 0), (half_kernel, half_kernel), (0, 0)))
    grad_masked = jnp.zeros_like(grad_mixed)
    for offset in range(kernel_len):
        start_row = 2 * half_kernel - offset
        grad_masked = (
            grad_masked
            + kernel_taps[offset] * grad_padded[:, start_row : start_row + frame_count, :]
        )
    grad_input = grad_stream + valid_rows * grad_masked
    terms = (
        kernel_term,
        conv_shift_term,
        scale_term,
        shift_term,
        up_term,
        up_offset_term,
        down_term,
        down_offset_term,
        gain_term,
    )
    return (grad_input, terms)


def body(
    frames,
    group,
    lengths,
    conv_weight,
    conv_bias,
    ada_scale,
    ada_shift,
    up_weight,
    up_bias,
    down_weight,
    down_bias,
    layer_scale,
    out_grad,
):
    stream = frames.astype(jnp.float32)
    frame_count = stream.shape[1]
    block_count = conv_weight.shape[0]
    valid_rows = (jnp.arange(frame_count, dtype=jnp.int32)[None, :] < lengths[:, None]).astype(
        jnp.float32
    )[:, :, None]
    select = (group[:, None] == jnp.arange(ada_scale.shape[1], dtype=jnp.int32)[None, :]).astype(
        jnp.float32
    )
    saved_states = []
    for block_index in range(block_count):
        fetched = (
            lax.all_gather(conv_weight[block_index], ("dp", "fsdp"), axis=1, tiled=True),
            lax.all_gather(conv_bias[block_index], ("dp", "fsdp"), axis=0, tiled=True),
            lax.all_gather(ada_scale[block_index], ("dp", "fsdp"), axis=1, tiled=True),
            lax.all_gather(ada_shift[block_index], ("dp", "fsdp"), axis=1, tiled=True),
            lax.all_gather(up_weight[block_index], ("dp", "fsdp"), axis=0, tiled=True),
            lax.all_gather(up_bias[block_index], ("dp", "fsdp"), axis=0, tiled=True),
            lax.all_gather(down_weight[block_index], ("dp", "fsdp"), axis=0, tiled=True),
            lax.all_gather(down_bias[block_index], ("dp", "fsdp"), axis=0, tiled=True),
            lax.all_gather(layer_scale[block_index], ("dp", "fsdp"), axis=0, tiled=True),
        )
        stream, block_state = forward_block(fetched, stream, valid_rows, select)
        saved_states.append(block_state)
    output = stream.astype(jnp.bfloat16)
    grad_stream = out_grad.astype(jnp.float32)
    shard_lists = [None] * block_count
    for block_index in reversed(range(block_count)):
        fetched = (
            lax.all_gather(conv_weight[block_index], ("dp", "fsdp"), axis=1, tiled=True),
            lax.all_gather(conv_bias[block_index], ("dp", "fsdp"), axis=0, tiled=True),
            lax.all_gather(ada_scale[block_index], ("dp", "fsdp"), axis=1, tiled=True),
            lax.all_gather(ada_shift[block_index], ("dp", "fsdp"), axis=1, tiled=True),
            lax.all_gather(up_weight[block_index], ("dp", "fsdp"), axis=0, tiled=True),
            lax.all_gather(up_bias[block_index], ("dp", "fsdp"), axis=0, tiled=True),
            lax.all_gather(down_weight[block_index], ("dp", "fsdp"), axis=0, tiled=True),
            lax.all_gather(down_bias[block_index], ("dp", "fsdp"), axis=0, tiled=True),
            lax.all_gather(layer_scale[block_index], ("dp", "fsdp"), axis=0, tiled=True),
        )
        grad_stream, terms = backward_block(
            fetched, saved_states[block_index], grad_stream, valid_rows, select
        )
        shards = (
            lax.psum_scatter(terms[0], ("dp", "fsdp"), scatter_dimension=1, tiled=True),
            lax.psum_scatter(terms[1], ("dp", "fsdp"), scatter_dimension=0, tiled=True),
            lax.psum_scatter(terms[2], ("dp", "fsdp"), scatter_dimension=1, tiled=True),
            lax.psum_scatter(terms[3], ("dp", "fsdp"), scatter_dimension=1, tiled=True),
            lax.psum_scatter(terms[4], ("dp", "fsdp"), scatter_dimension=0, tiled=True),
            lax.psum_scatter(terms[5], ("dp", "fsdp"), scatter_dimension=0, tiled=True),
            lax.psum_scatter(terms[6], ("dp", "fsdp"), scatter_dimension=0, tiled=True),
            lax.psum_scatter(terms[7], ("dp", "fsdp"), scatter_dimension=0, tiled=True),
            lax.psum_scatter(terms[8], ("dp", "fsdp"), scatter_dimension=0, tiled=True),
        )
        shard_lists[block_index] = shards
    stacked = tuple(
        (
            jnp.stack([shard_lists[block_index][entry] for block_index in range(block_count)])
            for entry in range(9)
        )
    )
    return (
        output,
        grad_stream,
        stacked[0],
        stacked[1],
        stacked[2],
        stacked[3],
        stacked[4],
        stacked[5],
        stacked[6],
        stacked[7],
        stacked[8],
    )


def solution(mesh):
    in_specs = (
        P(("dp", "fsdp"), None, None),
        P(("dp", "fsdp")),
        P(("dp", "fsdp")),
        P(None, None, ("dp", "fsdp")),
        P(None, ("dp", "fsdp")),
        P(None, None, ("dp", "fsdp")),
        P(None, None, ("dp", "fsdp")),
        P(None, ("dp", "fsdp"), None),
        P(None, ("dp", "fsdp")),
        P(None, ("dp", "fsdp"), None),
        P(None, ("dp", "fsdp")),
        P(None, ("dp", "fsdp")),
        P(("dp", "fsdp"), None, None),
    )
    out_specs = (
        P(("dp", "fsdp"), None, None),
        P(("dp", "fsdp"), None, None),
        P(None, None, ("dp", "fsdp")),
        P(None, ("dp", "fsdp")),
        P(None, None, ("dp", "fsdp")),
        P(None, None, ("dp", "fsdp")),
        P(None, ("dp", "fsdp"), None),
        P(None, ("dp", "fsdp")),
        P(None, ("dp", "fsdp"), None),
        P(None, ("dp", "fsdp")),
        P(None, ("dp", "fsdp")),
    )
    return jax.shard_map(body, mesh=mesh, in_specs=in_specs, out_specs=out_specs, check_vma=False)
```

profile of v0, /device:TPU:0, one launch (start us, length us, event | category | flops | bytes accessed | tf_op | source)
XLA Modules:
  0.0 1740.9 jit_solution(17593879401863547179)
XLA Ops:
  7.2 1.6 fusion.62
  8.9 1.5 fusion.61
  16.5 42.2 %all-reduce.21 = (bf16[512]{0:T(512)(128)(2,1)S(1)}, bf16[1536]{0:T(1024)(128)(2,1)S(1)}, bf16[512]{0:T(512)(128)(2,1)S(1)}, bf16[512]{0:T(512)(128)(2,1)S(1)}, ...) all-reduce(bf16[512]{0:T(512)(128)(2,1)S(1)} %dynamic-update-slice., ...), channel_id=3, replica_groups=mesh['dp'=4,'fsdp'=8] {'dp','fsdp'}, use_global_device_ids=true, to_apply=%add.5 | all-reduce | flops 6144 | bytes 24576
  59.6 41.4 %all-gather.2 = bf16[1,7,512]{1,0,2:T(2,128)(2,1)S(1)} all-gather(bf16[1,7,16]{1,0,2:T(2,128)(2,1)S(1)} %copy.55), channel_id=4, replica_groups=mesh['dp'=4,'fsdp'=8] {'dp','fsdp'}, dimensions={2}, use_global_device_ids=true | all-gather | bytes 7392 | tf_op jit(solution)/shard_map/all_gather | solution.py:137
  101.2 14.1 slice_reduce_fusion.13
  116.5 4.3 fusion.60
  120.9 1.9 copy-done
  123.8 37.3 %all-gather.3 = bf16[1,2,512]{1,0,2:T(2,128)(2,1)S(1)} all-gather(bf16[1,2,16]{1,0,2:T(2,128)(2,1)S(1)} %copy.56), channel_id=5, replica_groups=mesh['dp'=4,'fsdp'=8] {'dp','fsdp'}, dimensions={2}, use_global_device_ids=true | all-gather | bytes 2112 | tf_op jit(solution)/shard_map/all_gather | solution.py:139
  161.4 38.8 %all-gather.4 = bf16[1,2,512]{1,0,2:T(2,128)(2,1)S(1)} all-gather(bf16[1,2,16]{1,0,2:T(2,128)(2,1)S(1)} %copy.57), channel_id=6, replica_groups=mesh['dp'=4,'fsdp'=8] {'dp','fsdp'}, dimensions={2}, use_global_device_ids=true | all-gather | bytes 2112 | tf_op jit(solution)/shard_map/all_gather | solution.py:140
  200.9 37.7 %all-gather.11 = bf16[1,7,512]{1,0,2:T(2,128)(2,1)S(1)} all-gather(bf16[1,7,16]{1,0,2:T(2,128)(2,1)S(1)} %copy.58), channel_id=13, replica_groups=mesh['dp'=4,'fsdp'=8] {'dp','fsdp'}, dimensions={2}, use_global_device_ids=true | all-gather | bytes 7392 | tf_op jit(solution)/shard_map/all_gather | solution.py:137
  238.8 14.1 slice_reduce_fusion.6
  253.0 38.5 %all-gather.12 = bf16[1,2,512]{1,0,2:T(2,128)(2,1)S(1)} all-gather(bf16[1,2,16]{1,0,2:T(2,128)(2,1)S(1)} %copy.59), channel_id=14, replica_groups=mesh['dp'=4,'fsdp'=8] {'dp','fsdp'}, dimensions={2}, use_global_device_ids=true | all-gather | bytes 2112 | tf_op jit(solution)/shard_map/all_gather | solution.py:139
  292.0 37.6 %all-gather.13 = bf16[1,2,512]{1,0,2:T(2,128)(2,1)S(1)} all-gather(bf16[1,2,16]{1,0,2:T(2,128)(2,1)S(1)} %copy.60), channel_id=15, replica_groups=mesh['dp'=4,'fsdp'=8] {'dp','fsdp'}, dimensions={2}, use_global_device_ids=true | all-gather | bytes 2112 | tf_op jit(solution)/shard_map/all_gather | solution.py:140
  330.5 3.6 add_convert_fusion.3
  334.2 33.1 %multiply_convert_fusion.1 = (bf16[2048,1536]{1,0:T(8,128)(2,1)}, f32[2048,1536]{1,0:T(8,128)}, f32[2048,1536]{1,0:T(8,128)}) fusion(f32[1536]{0:T(1024)S(1)} %convert_element_type.134, bf16[2048,512]{1,0:T(8,128)(2,1)} %bitcast.165, bf16[1,512,1536]{2,1,0:T(8,128)(2,1)} %all-gather.23.cloned.1.call-done), kind=kOutput, calls=%fused_computation.21 | convolution fusion | flops 3428843520 | bytes 35133440 | tf_op jit(solution)/shard_map/dot_general | solution.py:35
  367.3 6.1 convolution_add_fusion.1
  373.5 3.2 convert_reduce_fusion.2
  376.6 3.8 fusion.58
  383.3 34.2 %multiply_convert_fusion = (bf16[2048,1536]{1,0:T(8,128)(2,1)}, f32[2048,1536]{1,0:T(8,128)}, f32[2048,1536]{1,0:T(8,128)}) fusion(f32[1536]{0:T(1024)S(1)} %convert_element_type.138, bf16[2048,512]{1,0:T(8,128)(2,1)S(1)} %bitcast.167, bf16[1,512,1536]{2,1,0:T(8,128)(2,1)} %all-gather.27.cloned.1.call-done), kind=kOutput, calls=%fused_computation.8 | convolution fusion | flops 3428843520 | bytes 35133440 | tf_op jit(solution)/shard_map/dot_general | solution.py:35
  417.5 14.7 convert_reduce_fusion
  432.3 3.5 fusion.18
  436.7 1.5 multiply_reduce_fusion.1
  438.3 20.4 %multiply_reduce_fusion.3 = (f32[512]{0:T(512)S(1)}, f32[512]{0:T(512)S(1)}, f32[512]{0:T(512)S(1)}, f32[512]{0:T(512)S(1)}, f32[512]{0:T(512)S(1)}, /*index=5*/...) fusion(f32[8,256,512]{2,1,0:T(8,128)} %copy-done.9, ...), kind=kLoop, calls=%fused_computation.60 | loop fusion | flops 23064576 | bytes 16842752 | tf_op jit(solution)/shard_map/reduce_sum | solution.py:83
  458.8 8.0 convolution_add_fusion
  466.8 20.3 %convert_reduce_fusion.3 = (f32[512]{0:T(512)S(1)}, bf16[8,256,512]{2,1,0:T(8,128)(2,1)}, f32[8,256,512]{2,1,0:T(8,128)}, bf16[8,256,512]{2,1,0:T(8,128)(2,1)}) fusion(f32[512]{0:T(512)S(1)} %convert_element_type.132, f32[8,256]{1,0:T(8,128)S(1)} %fusion.38, f32[512]{0:T(512)S(1)} %get-tuple-element.72, f32[512]{0:T(512)S(1)} %get-tuple-element.67, ...), kind=kLoop, calls=%fused_computation.57 | loop fusion | flops 29359616 | bytes 25194496 | tf_op jit(solution)/shard_map/reduce_sum | solution.py:54
  487.1 14.9 convert_reduce_fusion.1
  502.1 3.5 fusion.17
  506.5 1.5 multiply_reduce_fusion.2
  511.5 1.1 convolution_bitcast_fusion
  514.3 23.7 %multiply_reduce_fusion.10 = (f32[512]{0:T(512)S(1)}, f32[512]{0:T(512)S(1)}, f32[512]{0:T(512)S(1)}, f32[512]{0:T(512)S(1)}, f32[512]{0:T(512)S(1)}, /*index=5*...) fusion(f32[8,256,512]{2,1,0:T(8,128)} %copy-done.6, ...), kind=kLoop, calls=%fused_computation.67 | loop fusion | flops 32500736 | bytes 33632256 | tf_op jit(solution)/shard_map/reduce_sum | solution.py:83
  540.0 8.7 fusion.68
  548.9 7.9 fusion.69
  556.9 8.7 fusion.67
  565.7 7.9 fusion.66
  573.7 37.3 %all-reduce.20 = (f32[512]{0:T(512)S(1)}, f32[512]{0:T(512)S(1)}, f32[1536]{0:T(1024)S(1)}, f32[1536]{0:T(1024)S(1)}, f32[512]{0:T(512)S(1)}, /*index=5*/f32[512]{0:T(512)S(1)}, f32[512]{0:T(512)S(1)}, f32[512]{0:T(512)S(1)}) all-reduce(f32[512]{0:T(512)S(1)} %get-tuple-element.64, ...), channel_id=23, replica_groups=mesh['dp'=4,'fsdp'=8] {'dp','fsdp'}, use_global_device_ids=true, to_apply=%region_27.28.clone | all-reduce | flops 6144 | bytes 49152
  613.7 18.2 %multiply_add_fusion = f32[8,256,512]{2,1,0:T(8,128)} fusion(f32[8,256,512]{2,1,0:T(8,128)} %get-tuple-element.100, f32[8,256,512]{2,1,0:T(8,128)} %get-tuple-element.103, f32[512]{0:T(512)S(1)} %copy-done.39, f32[512]{0:T(512)S(1)} %copy-done.29, f32[512]{0:T(512)S(1)} %copy-done.31, f32[512]{0:T(512)S(1)} %copy-done.33, f32[512]{0:T(512)S(1)} %copy-done.35, ...), kind=kLoop, calls=%fused_computation.74 | loop fusion | flops 15728640 | bytes 12605440 | tf_op jit(solution)/shard_map/add | solution.py:95
  631.8 10.5 reduce-scatter.35.cloned.1.call-done
  643.1 132.8 %reduce-scatter.39.cloned.1.call-done = f32[16,2]{1,0:T(8,128)} async-done(((f32[512,2]{1,0:T(8,128)}), f32[16,2]{1,0:T(8,128)}) %reduce-scatter.39.cloned.1.call-update) | async-done | bytes 144
  776.7 133.0 %reduce-scatter.37.cloned.1.call-done = f32[16,2]{1,0:T(8,128)} async-done(((f32[512,2]{1,0:T(8,128)}), f32[16,2]{1,0:T(8,128)}) %reduce-scatter.37.cloned.1.call-update) | async-done | bytes 144
  910.4 132.6 %reduce-scatter.41.cloned.1.call-done = f32[16,2]{1,0:T(8,128)} async-done(((f32[512,2]{1,0:T(8,128)}), f32[16,2]{1,0:T(8,128)}) %reduce-scatter.41.cloned.1.call-update) | async-done | bytes 144
  1044.4 132.0 %reduce-scatter.31.cloned.1.call-done = f32[16,7]{1,0:T(8,128)} async-done(((f32[512,7]{1,0:T(8,128)}), f32[16,7]{1,0:T(8,128)}) %reduce-scatter.31.cloned.1.call-update) | async-done | bytes 464
  1177.1 132.4 %reduce-scatter.33.cloned.1.call-done = f32[16,7]{1,0:T(8,128)} async-done(((f32[512,7]{1,0:T(8,128)}), f32[16,7]{1,0:T(8,128)}) %reduce-scatter.33.cloned.1.call-update) | async-done | bytes 464
  1310.9 102.1 %reduce-scatter.27.cloned.1.call-done = f32[48,512]{1,0:T(8,128)} async-done(((f32[1536,512]{1,0:T(8,128)}), f32[48,512]{1,0:T(8,128)}) %reduce-scatter.27.cloned.1.call-update) | async-done | bytes 98320 | tf_op jit(solution)/shard_map/reduce_scatter | solution.py:174
  1413.0 106.4 %reduce-scatter.29.cloned.1.call-done = f32[48,512]{1,0:T(8,128)} async-done(((f32[1536,512]{1,0:T(8,128)}), f32[48,512]{1,0:T(8,128)}) %reduce-scatter.29.cloned.1.call-update) | async-done | bytes 98320 | tf_op jit(solution)/shard_map/reduce_scatter | solution.py:174
  1519.4 1.6 pad_maximum_fusion.1
  1521.0 105.0 %reduce-scatter.25.cloned.1.call-done = f32[16,1536]{1,0:T(8,128)} async-done(((f32[512,1536]{1,0:T(8,128)}), f32[16,1536]{1,0:T(8,128)}) %reduce-scatter.25.cloned.1.call-update) | async-done | bytes 98320 | tf_op jit(solution)/shard_map/reduce_scatter | solution.py:172
  1626.0 106.5 %reduce-scatter.23.cloned.1.call-done = f32[16,1536]{1,0:T(8,128)} async-done(((f32[512,1536]{1,0:T(8,128)}), f32[16,1536]{1,0:T(8,128)}) %reduce-scatter.23.cloned.1.call-update) | async-done | bytes 98320 | tf_op jit(solution)/shard_map/reduce_scatter | solution.py:172
  1732.5 1.6 pad_maximum_fusion
  (211 shorter events, 32.3 us)
Async XLA Ops:
  7.2 109.0 %copy-start.10 = (bf16[8,256,512]{2,1,0:T(8,128)(2,1)S(1)}, bf16[8,256,512]{2,1,0:T(8,128)(2,1)}, u32[]{:S(2)}) copy-start(bf16[8,256,512]{2,1,0:T(8,128)(2,1)} %param.13) | copy-start | bytes 6291460
  7.2 327.0 %all-gather.23.cloned.1.call-start = ((), (), s32[]{:S(2)}) async-start(), calls=%async_computation.14 | async-start | bytes 1622016 | tf_op jit(solution)/shard_map/all_gather | solution.py:141
  8.9 358.5 %all-gather.25.cloned.1.call-start = ((), (), s32[]{:S(2)}) async-start(), calls=%async_computation.15 | async-start | bytes 1622016 | tf_op jit(solution)/shard_map/all_gather | solution.py:143
  10.4 372.9 %all-gather.27.cloned.1.call-start = ((), (), s32[]{:S(2)}) async-start(), calls=%async_computation.16 | async-start | bytes 1622016 | tf_op jit(solution)/shard_map/all_gather | solution.py:141
  11.1 406.4 %all-gather.29.cloned.1.call-start = ((), (), s32[]{:S(2)}) async-start(), calls=%async_computation.17 | async-start | bytes 1622016 | tf_op jit(solution)/shard_map/all_gather | solution.py:143
  11.7 630.6 %reduce-scatter.35.cloned.1.call-start = ((), (), s32[]{:S(2)}) async-start(), calls=%async_computation.20 | async-start | bytes 270336
  115.3 5.5 copy-start.26
  115.4 5.5 copy-start.28
  115.4 5.5 copy-start.30
  115.4 5.5 copy-start.32
  115.4 5.5 copy-start.34
  115.4 5.5 copy-start.36
  115.4 5.5 copy-start.38
  120.9 40.4 %copy-start.45 = (bf16[2,2,16]{2,1,0:T(2,128)(2,1)S(1)}, bf16[2,2,16]{2,1,0:T(2,128)(2,1)}, u32[]{:S(2)}) copy-start(bf16[2,2,16]{2,1,0:T(2,128)(2,1)} %param.19) | copy-start | bytes 388
  120.9 79.4 %copy-start.40 = (s32[8]{0:T(128)S(1)}, s32[8]{0:T(128)}, u32[]{:S(2)}) copy-start(s32[8]{0:T(128)} %param.14) | copy-start | bytes 100
  120.9 209.6 %copy-start.22 = (f32[8,256]{1,0:T(8,128)}, f32[8,256]{1,0:T(8,128)S(1)}, u32[]{:S(2)}) copy-start(f32[8,256]{1,0:T(8,128)S(1)} %broadcast_multiply_fusion.5) | copy-start | bytes 24580
  123.7 210.4 %copy-start.24 = (f32[8,256]{1,0:T(8,128)}, f32[8,256]{1,0:T(8,128)S(1)}, u32[]{:S(2)}) copy-start(f32[8,256]{1,0:T(8,128)S(1)} %add_rsqrt_fusion.1) | copy-start | bytes 24580
  200.5 133.6 %copy-start.20 = (f32[8,512]{1,0:T(8,128)}, f32[8,512]{1,0:T(8,128)S(1)}, u32[]{:S(2)}) copy-start(f32[8,512]{1,0:T(8,128)S(1)} %fusion.42) | copy-start | bytes 49156
  367.3 6.1 copy-start.12
  383.3 34.2 %copy-start.16 = (bf16[8,256,512]{2,1,0:T(8,128)(2,1)}, bf16[8,256,512]{2,1,0:T(8,128)(2,1)S(1)}, u32[]{:S(2)}) copy-start(bf16[8,256,512]{2,1,0:T(8,128)(2,1)S(1)} %add_convert_fusion.2) | copy-start | bytes 6291460
  417.5 14.7 copy-start.19
  432.3 4.5 copy-start.3
  438.3 20.5 %copy-start.43 = (f32[512]{0:T(512)S(1)}, f32[512]{0:T(512)}, u32[]{:S(2)}) copy-start(f32[512]{0:T(512)} %convert_element_type.139) | copy-start | bytes 6148
  438.3 20.5 %copy-start.46 = (bf16[1,1536,512]{2,1,0:T(8,128)(2,1)S(1)}, bf16[1,1536,512]{2,1,0:T(8,128)(2,1)}, u32[]{:S(2)}) copy-start(bf16[1,1536,512]{2,1,0:T(8,128)(2,1)} %all-gather.29.cloned.1.call-done) | copy-start | bytes 4718596
  458.8 8.0 copy-start.8
  487.1 14.9 copy-start.18
  487.1 14.9 copy-start.21
  502.0 4.5 copy-start.1
  506.5 7.8 copy-start.11
  509.2 266.7 %reduce-scatter.39.cloned.1.call-start = ((), (), s32[]{:S(2)}) async-start(), calls=%async_computation.22 | async-start | bytes 270336
  512.7 397.0 %reduce-scatter.37.cloned.1.call-start = ((), (), s32[]{:S(2)}) async-start(), calls=%async_computation.21 | async-start | bytes 270336
  513.5 529.6 %reduce-scatter.41.cloned.1.call-start = ((), (), s32[]{:S(2)}) async-start(), calls=%async_computation.23 | async-start | bytes 270336
  514.2 662.1 %reduce-scatter.31.cloned.1.call-start = ((), (), s32[]{:S(2)}) async-start(), calls=%async_computation.18 | async-start | bytes 270336
  538.9 770.6 %reduce-scatter.33.cloned.1.call-start = ((), (), s32[]{:S(2)}) async-start(), calls=%async_computation.19 | async-start | bytes 270336
  539.9 9.0 copy-start.17
  539.9 873.1 %reduce-scatter.27.cloned.1.call-start = ((), (), s32[]{:S(2)}) async-start(), calls=%async_computation.12 | async-start | bytes 3244032 | tf_op jit(solution)/shard_map/reduce_scatter | solution.py:174
  548.7 970.7 %reduce-scatter.29.cloned.1.call-start = ((), (), s32[]{:S(2)}) async-start(), calls=%async_computation.13 | async-start | bytes 3244032 | tf_op jit(solution)/shard_map/reduce_scatter | solution.py:174
  556.8 8.9 copy-start.15
  556.8 1069.2 %reduce-scatter.25.cloned.1.call-start = ((), (), s32[]{:S(2)}) async-start(), calls=%async_computation.11 | async-start | bytes 3244032 | tf_op jit(solution)/shard_map/reduce_scatter | solution.py:172
  565.6 8.1 copy-start.42
  565.6 48.0 %copy-start.27 = (f32[512]{0:T(512)S(1)}, f32[512]{0:T(512)}, u32[]{:S(2)}) copy-start(f32[512]{0:T(512)} %copy-done.26) | copy-start | bytes 6148
  565.6 48.0 %copy-start.29 = (f32[512]{0:T(512)S(1)}, f32[512]{0:T(512)}, u32[]{:S(2)}) copy-start(f32[512]{0:T(512)} %copy-done.28) | copy-start | bytes 6148
  565.6 48.0 %copy-start.31 = (f32[512]{0:T(512)S(1)}, f32[512]{0:T(512)}, u32[]{:S(2)}) copy-start(f32[512]{0:T(512)} %copy-done.30) | copy-start | bytes 6148
  565.6 48.0 %copy-start.33 = (f32[512]{0:T(512)S(1)}, f32[512]{0:T(512)}, u32[]{:S(2)}) copy-start(f32[512]{0:T(512)} %copy-done.32) | copy-start | bytes 6148
  565.7 48.0 %copy-start.35 = (f32[512]{0:T(512)S(1)}, f32[512]{0:T(512)}, u32[]{:S(2)}) copy-start(f32[512]{0:T(512)} %copy-done.34) | copy-start | bytes 6148
  565.7 48.0 %copy-start.37 = (f32[512]{0:T(512)S(1)}, f32[512]{0:T(512)}, u32[]{:S(2)}) copy-start(f32[512]{0:T(512)} %copy-done.36) | copy-start | bytes 6148
  565.7 48.0 %copy-start.39 = (f32[512]{0:T(512)S(1)}, f32[512]{0:T(512)}, u32[]{:S(2)}) copy-start(f32[512]{0:T(512)} %copy-done.38) | copy-start | bytes 6148
  565.7 1166.8 %reduce-scatter.23.cloned.1.call-start = ((), (), s32[]{:S(2)}) async-start(), calls=%async_computation.10 | async-start | bytes 3244032 | tf_op jit(solution)/shard_map/reduce_scatter | solution.py:172
  (13 other events, 40.7 us)
Sparse Core Ops, SparseCore 0:
  11.4 57.6 all-gather.22
  72.0 54.0 all-gather.24
  129.5 54.0 all-gather.26
  186.9 54.2 all-gather.28
  509.3 132.9 reduce-scatter.34
  644.4 131.4 reduce-scatter.38
  778.1 131.4 reduce-scatter.36
  911.9 131.0 reduce-scatter.40
  1045.3 131.0 reduce-scatter.30
  1178.4 131.0 reduce-scatter.32
  1315.0 98.0 reduce-scatter.26
  1418.3 101.0 reduce-scatter.28
  1524.8 101.1 reduce-scatter.24
  1631.3 101.1 reduce-scatter.22
where the time goes:
time: 1740 us
  waiting for transfers between devices  1100 us (63%)
  blocking collectives  311 us (18%)
  matrix products  157 us (9%)
  other arithmetic  111 us (6%)
  local copies, waits for them, and re-layouts  50.3 us (3%)
    unnamed x20, waiting for transfers between devices  676 us
    reduce_scatter x2, waiting for transfers between devices, body(): lax.psum_scatter(terms[4], ('dp', 'fsdp'), scatter_dimension=0, tiled=True)  211 us
    reduce_scatter x2, waiting for transfers between devices, body(): lax.psum_scatter(terms[6], ('dp', 'fsdp'), scatter_dimension=0, tiled=True)  208 us
    unnamed x2, blocking collectives  79.5 us
    all_gather x2, blocking collectives, body(): lax.all_gather(conv_weight[block_index], ('dp', 'fsdp'), axis=1, tiled=True)  79 us
    all_gather x2, blocking collectives, body(): lax.all_gather(ada_shift[block_index], ('dp', 'fsdp'), axis=1, tiled=True)  76.5 us
    all_gather x2, blocking collectives, body(): lax.all_gather(ada_scale[block_index], ('dp', 'fsdp'), axis=1, tiled=True)  75.8 us
    dot_general x2, matrix products, forward_block(): jnp.dot(shaped_low, up_matrix, preferred_element_type=jnp.float32)  67.3 us
  transfers between devices with their start and end apart: 14, of which 10 were waited for; matrix products, arithmetic and copies ran while one was open for 13% of the time, Pallas kernels for 0%

commit v1 on v0

--- a/solution.py
+++ b/solution.py
@@ -5,6 +5,28 @@
 from jax.sharding import PartitionSpec as P
 
 EPSILON = 1e-06
+
+
+def laid_out(blocks, dim):
+    lengths = list(blocks.shape[1:])
+    lengths[dim] *= blocks.shape[0]
+    return jnp.moveaxis(blocks, 0, dim).reshape(lengths)
+
+
+def collected_by_bits(x, axis):
+    count = lax.axis_size(axis)
+    blocks = x[None]
+    for level in range(count.bit_length() - 1):
+        bit = 1 << level
+        received = lax.ppermute(blocks, axis, [(i, i ^ bit) for i in range(count)])
+        both = jnp.stack([blocks, received])
+        upper = lax.axis_index(axis) >> level & 1
+        blocks = jnp.where(upper == 0, both, both[::-1]).reshape(-1, *x.shape)
+    return blocks
+
+
+def doubled_up(shard, axis, dim):
+    return laid_out(collected_by_bits(shard, axis), dim)
 
 
 def forward_block(fetched, stream, valid_rows, select):
@@ -137,7 +159,7 @@
             lax.all_gather(conv_weight[block_index], ("dp", "fsdp"), axis=1, tiled=True),
             lax.all_gather(conv_bias[block_index], ("dp", "fsdp"), axis=0, tiled=True),
             lax.all_gather(ada_scale[block_index], ("dp", "fsdp"), axis=1, tiled=True),
-            lax.all_gather(ada_shift[block_index], ("dp", "fsdp"), axis=1, tiled=True),
+            doubled_up(ada_shift[block_index], ("dp", "fsdp"), 1),
             lax.all_gather(up_weight[block_index], ("dp", "fsdp"), axis=0, tiled=True),
             lax.all_gather(up_bias[block_index], ("dp", "fsdp"), axis=0, tiled=True),
             lax.all_gather(down_weight[block_index], ("dp", "fsdp"), axis=0, tiled=True),

time: 1740 us -> 1690 us (0.971)
  blocking collectives: 311 us -> 237 us
    all_gather x2 -> x0, blocking collectives: 76.5 us -> none  [body(): lax.all_gather(ada_shift[block_index], ('dp', 'fsdp'), axis=1, tiled=True)]
  transfers between devices with their start and end apart: 14 -> 24, of which waited for: 10 -> 18; matrix products, arithmetic and copies ran while one was open for 13% -> 13% of each run, Pallas kernels for 0% -> 0%
where the time goes in v1:
time: 1690 us; the launch traced here: 1680 us
  waiting for transfers between devices  1110 us (66%)
  blocking collectives  237 us (14%)
  matrix products  157 us (9%)
  other arithmetic  112 us (7%)
  local copies, waits for them, and re-layouts  50.7 us (3%)
    unnamed x20, waiting for transfers between devices  676 us
    reduce_scatter x2, waiting for transfers between devices, body(): lax.psum_scatter(terms[4], ('dp', 'fsdp'), scatter_dimension=0, tiled=True)  211 us
    reduce_scatter x2, waiting for transfers between devices, body(): lax.psum_scatter(terms[6], ('dp', 'fsdp'), scatter_dimension=0, tiled=True)  208 us
    unnamed x2, blocking collectives  81.2 us
    all_gather x2, blocking collectives, body(): lax.all_gather(conv_weight[block_index], ('dp', 'fsdp'), axis=1, tiled=True)  79.9 us
    all_gather x2, blocking collectives, body(): lax.all_gather(ada_scale[block_index], ('dp', 'fsdp'), axis=1, tiled=True)  75.6 us
    dot_general x2, matrix products, forward_block(): jnp.dot(shaped_low, up_matrix, preferred_element_type=jnp.float32)  67.3 us
    reduce_sum x2, other arithmetic, backward_block(): jnp.sum(grad_mixed * padded[:, offset:offset + frame_count, :], axis=(0, 1))  44.2 us
  transfers between devices with their start and end apart: 24, of which 18 were waited for; matrix products, arithmetic and copies ran while one was open for 13% of the time, Pallas kernels for 0%

profile of v1, /device:TPU:0, one launch (start us, length us, event | category | flops | bytes accessed | tf_op | source)
XLA Modules:
  0.0 1684.4 jit_solution(16016116655598984602)
XLA Ops:
  7.2 1.6 fusion.64
  17.2 42.3 %all-reduce.21 = (bf16[512]{0:T(512)(128)(2,1)S(1)}, bf16[1536]{0:T(1024)(128)(2,1)S(1)}, bf16[512]{0:T(512)(128)(2,1)S(1)}, bf16[512]{0:T(512)(128)(2,1)S(1)}, ...) all-reduce(bf16[512]{0:T(512)(128)(2,1)S(1)} %dynamic-update-slice., ...), channel_id=3, replica_groups=mesh['dp'=4,'fsdp'=8] {'dp','fsdp'}, use_global_device_ids=true, to_apply=%add.5 | all-reduce | flops 6144 | bytes 24576
  60.3 41.4 %all-gather.2 = bf16[1,7,512]{1,0,2:T(2,128)(2,1)S(1)} all-gather(bf16[1,7,16]{1,0,2:T(2,128)(2,1)S(1)} %copy.62), channel_id=4, replica_groups=mesh['dp'=4,'fsdp'=8] {'dp','fsdp'}, dimensions={2}, use_global_device_ids=true | all-gather | bytes 7392 | tf_op jit(solution)/shard_map/all_gather | solution.py:159
  102.0 14.1 slice_reduce_fusion.13
  117.3 4.3 fusion.62
  121.7 2.0 copy-done
  124.6 37.6 %all-gather.3 = bf16[1,2,512]{1,0,2:T(2,128)(2,1)S(1)} all-gather(bf16[1,2,16]{1,0,2:T(2,128)(2,1)S(1)} %copy.63), channel_id=5, replica_groups=mesh['dp'=4,'fsdp'=8] {'dp','fsdp'}, dimensions={2}, use_global_device_ids=true | all-gather | bytes 2112 | tf_op jit(solution)/shard_map/all_gather | solution.py:161
  162.5 38.5 %all-gather.10 = bf16[1,7,512]{1,0,2:T(2,128)(2,1)S(1)} all-gather(bf16[1,7,16]{1,0,2:T(2,128)(2,1)S(1)} %copy.64), channel_id=12, replica_groups=mesh['dp'=4,'fsdp'=8] {'dp','fsdp'}, dimensions={2}, use_global_device_ids=true | all-gather | bytes 7392 | tf_op jit(solution)/shard_map/all_gather | solution.py:159
  201.3 14.1 slice_reduce_fusion.6
  215.5 38.0 %all-gather.11 = bf16[1,2,512]{1,0,2:T(2,128)(2,1)S(1)} all-gather(bf16[1,2,16]{1,0,2:T(2,128)(2,1)S(1)} %copy.65), channel_id=13, replica_groups=mesh['dp'=4,'fsdp'=8] {'dp','fsdp'}, dimensions={2}, use_global_device_ids=true | all-gather | bytes 2112 | tf_op jit(solution)/shard_map/all_gather | solution.py:161
  260.5 1.5 collective-permute-done.2
  264.2 1.5 collective-permute-done.3
  267.2 1.6 collective-permute-start.9
  268.8 1.5 collective-permute-done.4
  272.1 3.6 add_convert_fusion.3
  275.8 33.1 %multiply_convert_fusion.1 = (bf16[2048,1536]{1,0:T(8,128)(2,1)}, f32[2048,1536]{1,0:T(8,128)}, f32[2048,1536]{1,0:T(8,128)}) fusion(f32[1536]{0:T(1024)S(1)} %convert_element_type.134, bf16[2048,512]{1,0:T(8,128)(2,1)} %bitcast.201, bf16[1,512,1536]{2,1,0:T(8,128)(2,1)} %all-gather.21.cloned.1.call-done), kind=kOutput, calls=%fused_computation.21 | convolution fusion | flops 3428843520 | bytes 35133440 | tf_op jit(solution)/shard_map/dot_general | solution.py:57
  308.9 6.1 convolution_add_fusion.1
  315.1 3.2 convert_reduce_fusion.2
  318.2 3.8 fusion.60
  324.9 34.2 %multiply_convert_fusion = (bf16[2048,1536]{1,0:T(8,128)(2,1)}, f32[2048,1536]{1,0:T(8,128)}, f32[2048,1536]{1,0:T(8,128)}) fusion(f32[1536]{0:T(1024)S(1)} %convert_element_type.138, bf16[2048,512]{1,0:T(8,128)(2,1)S(1)} %bitcast.203, bf16[1,512,1536]{2,1,0:T(8,128)(2,1)} %all-gather.25.cloned.1.call-done), kind=kOutput, calls=%fused_computation.8 | convolution fusion | flops 3428843520 | bytes 35133440 | tf_op jit(solution)/shard_map/dot_general | solution.py:57
  359.1 14.7 convert_reduce_fusion
  373.9 3.5 fusion.18
  378.3 1.5 multiply_reduce_fusion.1
  379.9 20.4 %multiply_reduce_fusion.3 = (f32[512]{0:T(512)S(1)}, f32[512]{0:T(512)S(1)}, f32[512]{0:T(512)S(1)}, f32[512]{0:T(512)S(1)}, f32[512]{0:T(512)S(1)}, /*index=5*/...) fusion(f32[8,256,512]{2,1,0:T(8,128)} %copy-done.9, ...), kind=kLoop, calls=%fused_computation.60 | loop fusion | flops 23064576 | bytes 16842752 | tf_op jit(solution)/shard_map/reduce_sum | solution.py:105
  400.4 8.0 convolution_add_fusion
  408.4 20.3 %convert_reduce_fusion.3 = (f32[512]{0:T(512)S(1)}, bf16[8,256,512]{2,1,0:T(8,128)(2,1)}, f32[8,256,512]{2,1,0:T(8,128)}, bf16[8,256,512]{2,1,0:T(8,128)(2,1)}) fusion(f32[512]{0:T(512)S(1)} %convert_element_type.132, f32[8,256]{1,0:T(8,128)S(1)} %fusion.38, f32[512]{0:T(512)S(1)} %get-tuple-element.83, f32[512]{0:T(512)S(1)} %get-tuple-element.78, ...), kind=kLoop, calls=%fused_computation.57 | loop fusion | flops 29359616 | bytes 25194496 | tf_op jit(solution)/shard_map/reduce_sum | solution.py:76
  428.7 14.9 convert_reduce_fusion.1
  443.7 3.5 fusion.17
  448.1 1.5 multiply_reduce_fusion.2
  455.9 23.7 %multiply_reduce_fusion.10 = (f32[512]{0:T(512)S(1)}, f32[512]{0:T(512)S(1)}, f32[512]{0:T(512)S(1)}, f32[512]{0:T(512)S(1)}, f32[512]{0:T(512)S(1)}, /*index=5*...) fusion(f32[8,256,512]{2,1,0:T(8,128)} %copy-done.6, ...), kind=kLoop, calls=%fused_computation.67 | loop fusion | flops 32500736 | bytes 33632256 | tf_op jit(solution)/shard_map/reduce_sum | solution.py:105
  481.6 8.7 fusion.69
  490.5 7.9 fusion.70
  498.5 8.7 fusion.68
  507.3 7.9 fusion.67
  515.3 38.9 %all-reduce.20 = (f32[512]{0:T(512)S(1)}, f32[512]{0:T(512)S(1)}, f32[1536]{0:T(1024)S(1)}, f32[1536]{0:T(1024)S(1)}, f32[512]{0:T(512)S(1)}, /*index=5*/f32[512]{0:T(512)S(1)}, f32[512]{0:T(512)S(1)}, f32[512]{0:T(512)S(1)}) all-reduce(f32[512]{0:T(512)S(1)} %get-tuple-element.75, ...), channel_id=21, replica_groups=mesh['dp'=4,'fsdp'=8] {'dp','fsdp'}, use_global_device_ids=true, to_apply=%region_27.28.clone | all-reduce | flops 6144 | bytes 49152
  556.9 18.2 %multiply_add_fusion = f32[8,256,512]{2,1,0:T(8,128)} fusion(f32[8,256,512]{2,1,0:T(8,128)} %get-tuple-element.111, f32[8,256,512]{2,1,0:T(8,128)} %get-tuple-element.114, f32[512]{0:T(512)S(1)} %copy-done.39, f32[512]{0:T(512)S(1)} %copy-done.29, f32[512]{0:T(512)S(1)} %copy-done.31, f32[512]{0:T(512)S(1)} %copy-done.33, f32[512]{0:T(512)S(1)} %copy-done.35, ...), kind=kLoop, calls=%fused_computation.74 | loop fusion | flops 15728640 | bytes 12605440 | tf_op jit(solution)/shard_map/add | solution.py:117
  575.0 9.7 reduce-scatter.35.cloned.1.call-done
  585.5 132.9 %reduce-scatter.39.cloned.1.call-done = f32[16,2]{1,0:T(8,128)} async-done(((f32[512,2]{1,0:T(8,128)}), f32[16,2]{1,0:T(8,128)}) %reduce-scatter.39.cloned.1.call-update) | async-done | bytes 144
  719.2 133.0 %reduce-scatter.37.cloned.1.call-done = f32[16,2]{1,0:T(8,128)} async-done(((f32[512,2]{1,0:T(8,128)}), f32[16,2]{1,0:T(8,128)}) %reduce-scatter.37.cloned.1.call-update) | async-done | bytes 144
  852.9 133.0 %reduce-scatter.41.cloned.1.call-done = f32[16,2]{1,0:T(8,128)} async-done(((f32[512,2]{1,0:T(8,128)}), f32[16,2]{1,0:T(8,128)}) %reduce-scatter.41.cloned.1.call-update) | async-done | bytes 144
  987.3 132.4 %reduce-scatter.31.cloned.1.call-done = f32[16,7]{1,0:T(8,128)} async-done(((f32[512,7]{1,0:T(8,128)}), f32[16,7]{1,0:T(8,128)}) %reduce-scatter.31.cloned.1.call-update) | async-done | bytes 464
  1120.4 132.8 %reduce-scatter.33.cloned.1.call-done = f32[16,7]{1,0:T(8,128)} async-done(((f32[512,7]{1,0:T(8,128)}), f32[16,7]{1,0:T(8,128)}) %reduce-scatter.33.cloned.1.call-update) | async-done | bytes 464
  1254.6 102.0 %reduce-scatter.27.cloned.1.call-done = f32[48,512]{1,0:T(8,128)} async-done(((f32[1536,512]{1,0:T(8,128)}), f32[48,512]{1,0:T(8,128)}) %reduce-scatter.27.cloned.1.call-update) | async-done | bytes 98320 | tf_op jit(solution)/shard_map/reduce_scatter | solution.py:196
  1356.6 106.4 %reduce-scatter.29.cloned.1.call-done = f32[48,512]{1,0:T(8,128)} async-done(((f32[1536,512]{1,0:T(8,128)}), f32[48,512]{1,0:T(8,128)}) %reduce-scatter.29.cloned.1.call-update) | async-done | bytes 98320 | tf_op jit(solution)/shard_map/reduce_scatter | solution.py:196
  1463.0 1.6 pad_maximum_fusion.1
  1464.7 104.9 %reduce-scatter.25.cloned.1.call-done = f32[16,1536]{1,0:T(8,128)} async-done(((f32[512,1536]{1,0:T(8,128)}), f32[16,1536]{1,0:T(8,128)}) %reduce-scatter.25.cloned.1.call-update) | async-done | bytes 98320 | tf_op jit(solution)/shard_map/reduce_scatter | solution.py:194
  1569.6 106.4 %reduce-scatter.23.cloned.1.call-done = f32[16,1536]{1,0:T(8,128)} async-done(((f32[512,1536]{1,0:T(8,128)}), f32[16,1536]{1,0:T(8,128)}) %reduce-scatter.23.cloned.1.call-update) | async-done | bytes 98320 | tf_op jit(solution)/shard_map/reduce_scatter | solution.py:194
  1676.0 1.6 pad_maximum_fusion
  (249 shorter events, 46.1 us)
Async XLA Ops:
  7.2 109.7 %copy-start.10 = (bf16[8,256,512]{2,1,0:T(8,128)(2,1)S(1)}, bf16[8,256,512]{2,1,0:T(8,128)(2,1)}, u32[]{:S(2)}) copy-start(bf16[8,256,512]{2,1,0:T(8,128)(2,1)} %param.13) | copy-start | bytes 6291460
  7.2 268.6 %all-gather.21.cloned.1.call-start = ((), (), s32[]{:S(2)}) async-start(), calls=%async_computation.14 | async-start | bytes 1622016 | tf_op jit(solution)/shard_map/all_gather | solution.py:163
  8.9 300.0 %all-gather.23.cloned.1.call-start = ((), (), s32[]{:S(2)}) async-start(), calls=%async_computation.15 | async-start | bytes 1622016 | tf_op jit(solution)/shard_map/all_gather | solution.py:165
  10.4 314.5 %all-gather.25.cloned.1.call-start = ((), (), s32[]{:S(2)}) async-start(), calls=%async_computation.16 | async-start | bytes 1622016 | tf_op jit(solution)/shard_map/all_gather | solution.py:163
  11.1 348.0 %all-gather.27.cloned.1.call-start = ((), (), s32[]{:S(2)}) async-start(), calls=%async_computation.17 | async-start | bytes 1622016 | tf_op jit(solution)/shard_map/all_gather | solution.py:165
  11.9 242.7 %collective-permute-start = (bf16[1,2,16]{2,1,0:T(2,128)(2,1)S(1)}, bf16[1,2,16]{2,1,0:T(2,128)(2,1)S(1)}, u32[]{:S(2)}, u32[]{:S(2)}) collective-permute-start(bf16[1,2,16]{2,1,0:T(2,128)(2,1)S(1)} %get-tuple-element.139), channel_id=1, source_target_pairs={{0,1},{1,0},{2,3},{3,2},{4,5},{5,4},{6,7},{7,6},{8,9},{9,8},{10,11... | collective-permute-start | bytes 200 | tf_op jit(solution)/shard_map/ppermute | solution.py:21
  12.4 243.7 %collective-permute-start.5 = (bf16[1,2,16]{2,1,0:T(2,128)(2,1)S(1)}, bf16[1,2,16]{2,1,0:T(2,128)(2,1)S(1)}, u32[]{:S(2)}, u32[]{:S(2)}) collective-permute-start(bf16[1,2,16]{2,1,0:T(2,128)(2,1)S(1)} %get-tuple-element.138), channel_id=1, source_target_pairs={{0,1},{1,0},{2,3},{3,2},{4,5},{5,4},{6,7},{7,6},{8,9},{9,8},{10,11... | collective-permute-start | bytes 200 | tf_op jit(solution)/shard_map/ppermute | solution.py:21
  12.4 572.3 %reduce-scatter.35.cloned.1.call-start = ((), (), s32[]{:S(2)}) async-start(), calls=%async_computation.20 | async-start | bytes 270336
  121.7 132.0 %copy-start.40 = (s32[8]{0:T(128)S(1)}, s32[8]{0:T(128)}, u32[]{:S(2)}) copy-start(s32[8]{0:T(128)} %param.14) | copy-start | bytes 100
  121.7 150.4 %copy-start.22 = (f32[8,256]{1,0:T(8,128)}, f32[8,256]{1,0:T(8,128)S(1)}, u32[]{:S(2)}) copy-start(f32[8,256]{1,0:T(8,128)S(1)} %broadcast_multiply_fusion.5) | copy-start | bytes 24580
  124.5 151.3 %copy-start.24 = (f32[8,256]{1,0:T(8,128)}, f32[8,256]{1,0:T(8,128)S(1)}, u32[]{:S(2)}) copy-start(f32[8,256]{1,0:T(8,128)S(1)} %add_rsqrt_fusion.1) | copy-start | bytes 24580
  253.8 55.1 %copy-start.20 = (f32[8,512]{1,0:T(8,128)}, f32[8,512]{1,0:T(8,128)S(1)}, u32[]{:S(2)}) copy-start(f32[8,512]{1,0:T(8,128)S(1)} %fusion.42) | copy-start | bytes 49156
  254.6 3.6 collective-permute-start.1
  256.1 3.6 collective-permute-start.6
  258.3 3.7 collective-permute-start.2
  259.8 3.7 collective-permute-start.7
  262.0 3.7 collective-permute-start.3
  263.5 3.7 collective-permute-start.8
  265.7 4.6 collective-permute-start.4
  267.2 4.6 collective-permute-start.9
  308.9 6.1 copy-start.12
  324.9 34.2 %copy-start.16 = (bf16[8,256,512]{2,1,0:T(8,128)(2,1)}, bf16[8,256,512]{2,1,0:T(8,128)(2,1)S(1)}, u32[]{:S(2)}) copy-start(bf16[8,256,512]{2,1,0:T(8,128)(2,1)S(1)} %add_convert_fusion.2) | copy-start | bytes 6291460
  359.1 14.7 copy-start.19
  379.9 20.5 %copy-start.43 = (f32[512]{0:T(512)S(1)}, f32[512]{0:T(512)}, u32[]{:S(2)}) copy-start(f32[512]{0:T(512)} %convert_element_type.139) | copy-start | bytes 6148
  379.9 20.5 %copy-start.45 = (bf16[1,1536,512]{2,1,0:T(8,128)(2,1)S(1)}, bf16[1,1536,512]{2,1,0:T(8,128)(2,1)}, u32[]{:S(2)}) copy-start(bf16[1,1536,512]{2,1,0:T(8,128)(2,1)} %all-gather.27.cloned.1.call-done) | copy-start | bytes 4718596
  400.4 8.0 copy-start.8
  428.7 14.9 copy-start.18
  428.7 14.9 copy-start.21
  448.1 7.8 copy-start.11
  450.8 267.6 %reduce-scatter.39.cloned.1.call-start = ((), (), s32[]{:S(2)}) async-start(), calls=%async_computation.22 | async-start | bytes 270336
  454.3 397.9 %reduce-scatter.37.cloned.1.call-start = ((), (), s32[]{:S(2)}) async-start(), calls=%async_computation.21 | async-start | bytes 270336
  455.1 530.8 %reduce-scatter.41.cloned.1.call-start = ((), (), s32[]{:S(2)}) async-start(), calls=%async_computation.23 | async-start | bytes 270336
  455.8 663.9 %reduce-scatter.31.cloned.1.call-start = ((), (), s32[]{:S(2)}) async-start(), calls=%async_computation.18 | async-start | bytes 270336
  480.5 772.7 %reduce-scatter.33.cloned.1.call-start = ((), (), s32[]{:S(2)}) async-start(), calls=%async_computation.19 | async-start | bytes 270336
  481.5 9.0 copy-start.17
  481.5 875.1 %reduce-scatter.27.cloned.1.call-start = ((), (), s32[]{:S(2)}) async-start(), calls=%async_computation.12 | async-start | bytes 3244032 | tf_op jit(solution)/shard_map/reduce_scatter | solution.py:196
  490.3 972.8 %reduce-scatter.29.cloned.1.call-start = ((), (), s32[]{:S(2)}) async-start(), calls=%async_computation.13 | async-start | bytes 3244032 | tf_op jit(solution)/shard_map/reduce_scatter | solution.py:196
  498.4 8.9 copy-start.15
  498.4 1071.1 %reduce-scatter.25.cloned.1.call-start = ((), (), s32[]{:S(2)}) async-start(), calls=%async_computation.11 | async-start | bytes 3244032 | tf_op jit(solution)/shard_map/reduce_scatter | solution.py:194
  507.2 8.1 copy-start.42
  507.2 49.6 %copy-start.27 = (f32[512]{0:T(512)S(1)}, f32[512]{0:T(512)}, u32[]{:S(2)}) copy-start(f32[512]{0:T(512)} %copy-done.26) | copy-start | bytes 6148
  507.2 49.6 %copy-start.29 = (f32[512]{0:T(512)S(1)}, f32[512]{0:T(512)}, u32[]{:S(2)}) copy-start(f32[512]{0:T(512)} %copy-done.28) | copy-start | bytes 6148
  507.2 49.6 %copy-start.31 = (f32[512]{0:T(512)S(1)}, f32[512]{0:T(512)}, u32[]{:S(2)}) copy-start(f32[512]{0:T(512)} %copy-done.30) | copy-start | bytes 6148
  507.2 49.6 %copy-start.33 = (f32[512]{0:T(512)S(1)}, f32[512]{0:T(512)}, u32[]{:S(2)}) copy-start(f32[512]{0:T(512)} %copy-done.32) | copy-start | bytes 6148
  507.3 49.6 %copy-start.35 = (f32[512]{0:T(512)S(1)}, f32[512]{0:T(512)}, u32[]{:S(2)}) copy-start(f32[512]{0:T(512)} %copy-done.34) | copy-start | bytes 6148
  507.3 49.6 %copy-start.37 = (f32[512]{0:T(512)S(1)}, f32[512]{0:T(512)}, u32[]{:S(2)}) copy-start(f32[512]{0:T(512)} %copy-done.36) | copy-start | bytes 6148
  507.3 49.6 %copy-start.39 = (f32[512]{0:T(512)S(1)}, f32[512]{0:T(512)}, u32[]{:S(2)}) copy-start(f32[512]{0:T(512)} %copy-done.38) | copy-start | bytes 6148
  507.3 1168.7 %reduce-scatter.23.cloned.1.call-start = ((), (), s32[]{:S(2)}) async-start(), calls=%async_computation.10 | async-start | bytes 3244032 | tf_op jit(solution)/shard_map/reduce_scatter | solution.py:194
  (22 other events, 87.7 us)
Sparse Core Ops, SparseCore 0:
  11.4 57.6 all-gather.20
  72.0 53.9 all-gather.22
  129.4 54.2 all-gather.24
  187.0 53.7 all-gather.26
  450.9 133.7 reduce-scatter.34
  586.8 131.5 reduce-scatter.38
  720.6 131.4 reduce-scatter.36
  854.4 131.4 reduce-scatter.40
  988.1 131.4 reduce-scatter.30
  1121.7 131.4 reduce-scatter.32
  1258.7 97.9 reduce-scatter.26
  1361.9 101.0 reduce-scatter.28
  1468.5 101.0 reduce-scatter.24
  1574.9 101.0 reduce-scatter.22
